TPU v7x, 32 devices: a whole 2x2x4 slice. The times are simulated.
32 devices in a mesh: groups: 2 (over y), depth: 4 (over z), rows: 2 (over x), cols: 2 (over core).
Axes of the slice: x: 2, y: 2, z: 4, core: 2. Of those that a mesh axis runs over, the one named last changes fastest.
Arguments:
- volume: bfloat16 [4, 16, 16, 3072], P('groups', 'depth', 'rows', 'cols'), parts along dimension 0, may hold values from -6 to 6
- grad_out: bfloat16 [4, 16, 16, 3072], P('groups', 'depth', 'rows', 'cols'), parts along dimension 0, may hold values from -6 to 6
- report: bfloat16 [1536], P('groups'), parts along dimension 0, may hold values from -6 to 6
- conv_kernel: bfloat16 [96, 1, 7, 7, 7], replicated, may hold values from -0.3125 to 0.3125
- conv_bias: float32 [96], replicated, may hold values from -4 to 4
- film_weight: bfloat16 [768, 192], replicated, may hold values from -0.21875 to 0.21875
- film_bias: float32 [192], replicated, may hold values from -3 to 3
- in_weight: bfloat16 [96, 384], replicated, may hold values from -0.625 to 0.625
- in_bias: float32 [384], replicated, may hold values from -3 to 3
- out_weight: bfloat16 [384, 96], replicated, may hold values from -0.3125 to 0.3125
Outputs:
- grad_input: bfloat16 [4, 16, 16, 3072], P('groups', 'depth', 'rows', 'cols'), parts along dimension 0
- grad_kernel: float32 [192, 1, 7, 7, 7], P('groups'), parts along dimension 0
- grad_conv_bias: float32 [192], P('groups'), parts along dimension 0
- grad_film: float32 [384], P('groups'), parts along dimension 0
- grad_in_weight: float32 [192, 384], P('groups'), parts along dimension 0
- grad_in_bias: float32 [768], P('groups'), parts along dimension 0
- grad_out_weight: float32 [768, 96], P('groups'), parts along dimension 0
There are 2 independent parts, one for each index of `groups`. A program takes and returns all parts, laid end to end along the dimension named above; an argument that names none is the same for every part. Nothing has to cross between parts.
All inputs are finite; a program needn't handle non-finite values.
Results may differ from a plain program's by a relative error of at most 0.0062.
Values may be sent and summed in bfloat16 or wider, within the bound.
A program may use at most 64 MiB of HBM per device.

v0:
```python
import math

import jax
import jax.numpy as jnp
from jax import lax
from jax.sharding import PartitionSpec as P

K = 7


epsilon = 1e-06
last_dims = ("NDHWC", "OIDHW", "NDHWC")
grad_dims = ("NDHWC", "DHWIO", "NDHWC")


def padded_2(block, sides, width):
    for axis, dim in sides:
        count = lax.axis_size(axis)
        forward = [(i, i + 1) for i in range(count - 1)]
        backward = [(target, source) for source, target in forward]
        low = lax.ppermute(
            lax.slice_in_dim(block, block.shape[dim] - width, None, axis=dim), axis, forward
        )
        high = lax.ppermute(lax.slice_in_dim(block, 0, width, axis=dim), axis, backward)
        block = jnp.concatenate([low, block, high], axis=dim)
    return block


def depthwise(padded, kernel):
    return lax.conv_general_dilated(
        padded,
        kernel,
        (1, 1, 1),
        "VALID",
        dimension_numbers=last_dims,
        feature_group_count=kernel.shape[0],
        preferred_element_type=jnp.float32,
    )


def widen(field):
    half_width = K // 2
    result = padded_2(field, (("depth", 1), ("rows", 2), ("cols", 3)), half_width)
    return result


def pointwise(conv_flat, grad_flat, film_vec, in_weight, in_bias, out_weight):
    channels = conv_flat.shape[0]
    chan_mean = jnp.mean(conv_flat, axis=0)
    centred = conv_flat - chan_mean
    variance = jnp.mean(centred * centred, axis=0)
    inverse = lax.rsqrt(variance + epsilon)
    normed = centred * inverse
    scale_vec = 1.0 + film_vec[:channels, None]
    hidden_in = (normed * scale_vec + film_vec[channels:, None]).astype(jnp.bfloat16)
    pre_act = jnp.dot(in_weight.T, hidden_in, preferred_element_type=jnp.float32) + in_bias[:, None]
    post_act, gelu_back = jax.vjp(jax.nn.gelu, pre_act)
    act_low = post_act.astype(jnp.bfloat16)
    grad_act = jnp.dot(out_weight, grad_flat, preferred_element_type=jnp.float32)
    grad_pre = gelu_back(grad_act)[0]
    grad_low = grad_pre.astype(jnp.bfloat16)
    grad_hidden = jnp.dot(in_weight, grad_low, preferred_element_type=jnp.float32)
    grad_out_w = jnp.dot(act_low, grad_flat.T, preferred_element_type=jnp.float32)
    grad_in_w = jnp.dot(hidden_in, grad_low.T, preferred_element_type=jnp.float32)
    grad_in_b = jnp.sum(grad_pre, axis=1)
    grad_film = jnp.concatenate(
        [jnp.sum(grad_hidden * normed, axis=1), jnp.sum(grad_hidden, axis=1)]
    )
    grad_normed = grad_hidden * scale_vec
    slope = (
        (
            grad_normed
            - jnp.mean(grad_normed, axis=0)
            - normed * jnp.mean(grad_normed * normed, axis=0)
        )
        * inverse
    ).astype(jnp.bfloat16)
    return (slope, (grad_in_w, grad_in_b, grad_out_w, grad_film))


def local(
    volume,
    grad_out,
    report,
    conv_kernel,
    conv_bias,
    film_weight,
    film_bias,
    in_weight,
    in_bias,
    out_weight,
):
    crops, slices, lines, merged = volume.shape
    channels = conv_kernel.shape[0]
    local_shape = (crops, slices, lines, merged // channels, channels)
    film_vec = (
        jnp.dot(report[None, :], film_weight, preferred_element_type=jnp.float32)[0] + film_bias
    )
    local_vol = volume.reshape(local_shape)
    local_grad = grad_out.reshape(local_shape)
    padded = widen(local_vol)
    conv_out = depthwise(padded, conv_kernel) + conv_bias
    conv_flat = conv_out.reshape(-1, channels).T
    grad_flat = local_grad.reshape(-1, channels).T
    slope_flat, local_grads = pointwise(
        conv_flat, grad_flat, film_vec, in_weight, in_bias, out_weight
    )
    voxel_count = (
        conv_flat.shape[1] * lax.axis_size("depth") * lax.axis_size("rows") * lax.axis_size("cols")
    )
    factor = 1.0 / math.sqrt(voxel_count)
    term_in_w = local_grads[0] * factor
    term_in_b = local_grads[1] * factor
    term_out_w = local_grads[2] * factor
    term_film = local_grads[3] * factor
    summed_mlp = lax.psum((term_in_w, term_in_b, term_out_w, term_film), ("depth", "rows", "cols"))
    slope_vol = slope_flat.T.reshape(local_shape)
    slope_pad = widen(slope_vol)
    flipped = conv_kernel[:, :, ::-1, ::-1, ::-1]
    grad_input = (
        (local_grad.astype(jnp.float32) + depthwise(slope_pad, flipped))
        .astype(jnp.bfloat16)
        .reshape(volume.shape)
    )
    kernel_local = jnp.zeros((1, K, K, K, channels), jnp.float32)
    for crop_index in range(crops):
        kernel_local = kernel_local + lax.conv_general_dilated(
            padded[crop_index][None],
            slope_vol[crop_index][:, :, :, None, :],
            (1, 1, 1),
            "VALID",
            dimension_numbers=grad_dims,
            feature_group_count=channels,
            preferred_element_type=jnp.float32,
        )
    term_kernel = jnp.moveaxis(kernel_local[0], 3, 0)[:, None] * factor
    term_bias = jnp.sum(slope_flat.astype(jnp.float32), axis=1) * factor
    summed_conv = lax.psum((term_kernel, term_bias), ("depth", "rows", "cols"))
    totals = tuple(summed_mlp) + tuple(summed_conv)
    return (grad_input, totals[4], totals[5], totals[3], totals[0], totals[1], totals[2])


def solution(mesh):
    in_specs = (
        P("groups", "depth", "rows", "cols"),
        P("groups", "depth", "rows", "cols"),
        P("groups"),
        P(),
        P(),
        P(),
        P(),
        P(),
        P(),
        P(),
    )
    out_specs = (
        P("groups", "depth", "rows", "cols"),
        P("groups", None, None, None, None),
        P("groups"),
        P("groups"),
        P("groups", None),
        P("groups"),
        P("groups", None),
    )
    return jax.shard_map(local, mesh=mesh, in_specs=in_specs, out_specs=out_specs, check_vma=False)
```

profile of v0, /device:TPU:1, one launch (start us, length us, event | category | flops | bytes accessed | tf_op | source)
XLA Modules:
  0.0 244.7 jit_solution(1171630249008193471)
XLA Ops:
  7.2 1.2 reshape.65
  8.5 0.2 copy.119
  8.8 4.0 %collective-permute-start = (bf16[2,3,8,16,96]{4,0,3,2,1:T(2,128)(2,1)S(1)}, bf16[2,3,8,16,96]{4,0,3,2,1:T(2,128)(2,1)S(1)}, u32[]{:S(2)}, u32[]{:S(2)}) collective-permute-start(bf16[2,3,8,16,96]{4,0,3,2,1:T(2,128)(2,1)S(1)} %copy.119), channel_id=1, source_target_pairs={{0,4},{4,8},{8,12},{1,5},{5,9},{9,13},{2,6},{6,10},{10,14},{3,7},{... | collective-permute-start | bytes 442376 | tf_op jit(solution)/shard_map/ppermute | solution.py:21
  12.8 0.2 copy.120
  13.0 1.3 collective-permute-start.1
  14.3 0.2 reshape_reshape.3
  14.6 0.2 reshape.69
  14.8 1.6 collective-permute-done
  16.3 0.1 constant_dynamic-update-slice_fusion.2
  16.5 0.3 constant_dynamic-update-slice_fusion.1
  16.8 3.6 %collective-permute-done.1 = bf16[2,3,8,16,96]{4,0,3,2,1:T(2,128)(2,1)S(1)} collective-permute-done((bf16[2,3,8,16,96]{4,0,3,2,1:T(2,128)(2,1)S(1)}, bf16[2,3,8,16,96]{4,0,3,2,1:T(2,128)(2,1)S(1)}, u32[]{:S(2)}, u32[]{:S(2)}) %collective-permute-start.1) | collective-permute-done | bytes 147488 | tf_op jit(solution)/shard_map/ppermute | solution.py:24
  20.4 0.2 constant_dynamic-update-slice_fusion
  20.6 0.4 fusion.54
  20.9 3.1 %collective-permute-start.2 = (bf16[2,10,3,16,96]{4,0,3,2,1:T(2,128)(2,1)S(1)}, bf16[2,10,3,16,96]{4,0,3,2,1:T(2,128)(2,1)S(1)}, u32[]{:S(2)}, u32[]{:S(2)}) collective-permute-start(bf16[2,10,3,16,96]{4,0,3,2,1:T(2,128)(2,1)S(1)} %get-tuple-element.57), channel_id=1, source_target_pairs={{0,2},{1,3},{4,6},{5,7},{8,10},{9,11},{12,14},{13,15},{16,18},{17,... | collective-permute-start | bytes 552968 | tf_op jit(solution)/shard_map/ppermute | solution.py:21
  24.1 1.3 collective-permute-start.3
  25.4 0.1 fusion.61
  25.5 2.0 collective-permute-done.2
  27.5 3.8 %collective-permute-done.3 = bf16[2,10,3,16,96]{4,0,3,2,1:T(2,128)(2,1)S(1)} collective-permute-done((bf16[2,10,3,16,96]{4,0,3,2,1:T(2,128)(2,1)S(1)}, bf16[2,10,3,16,96]{4,0,3,2,1:T(2,128)(2,1)S(1)}, u32[]{:S(2)}, u32[]{:S(2)}) %collective-permute-start.3) | collective-permute-done | bytes 184352 | tf_op jit(solution)/shard_map/ppermute | solution.py:24
  31.4 0.7 pad_maximum_fusion.6
  32.1 1.3 collective-permute-start.4
  33.4 5.1 %collective-permute-start.5 = (bf16[2,10,14,3,96]{4,0,3,2,1:T(2,128)(2,1)S(1)}, bf16[2,10,14,3,96]{4,0,3,2,1:T(2,128)(2,1)S(1)}, u32[]{:S(2)}, u32[]{:S(2)}) collective-permute-start(bf16[2,10,14,3,96]{4,0,3,2,1:T(2,128)(2,1)S(1)} %get-tuple-element.54), channel_id=1, source_target_pairs={{1,0},{3,2},{5,4},{7,6},{9,8},{11,10},{13,12},{15,14},{17,16},{19,... | collective-permute-start | bytes 483848 | tf_op jit(solution)/shard_map/ppermute | solution.py:24
  38.6 0.8 collective-permute-done.5
  39.3 7.8 %pad_maximum_fusion = bf16[2,10,14,22,96]{4,0,3,2,1:T(2,128)(2,1)S(1)} fusion(bf16[2,10,14,3,96]{4,0,3,2,1:T(2,128)(2,1)S(1)} %collective-permute-done.5, bf16[2,10,3,16,96]{4,0,3,2,1:T(2,128)(2,1)S(1)} %collective-permute-done.3, bf16[2,10,8,16,96]{4,0,3,2,1:T(2,128)(2,1)S(1)} %constant_dynamic-update-slice_fusion, ...), kind=kLoop, calls=%fused_computation.6 | loop fusion | flops 2365440 | bytes 2365440 | tf_op jit(solution)/shard_map/concatenate | solution.py:25
  47.1 19.1 %fusion.59 = (f32[2,4,8,16]{0,3,2,1:T(8,128)S(1)}, f32[2,4,8,16,96]{4,0,3,2,1:T(2,128)S(1)}) fusion(f32[96]{0:T(128)S(1)} %copy-done.13, bf16[2,10,14,22,96]{4,0,3,2,1:T(2,128)(2,1)S(1)} %pad_maximum_fusion, bf16[96,1,7,7,7]{0,4,3,2,1:T(8,128)(2,1)S(1)} %copy-done.10), kind=kOutput, calls=%fused_computation.92 | convolution fusion | flops 67632128 | bytes 1646272 | tf_op jit(solution)/shard_map/conv_general_dilated | solution.py:30
  66.3 0.2 copy.90
  66.5 0.3 copy.89
  66.8 0.1 div.15
  66.9 0.2 copy-done.4
  67.1 0.5 convolution_add_fusion
  67.6 1.3 convolution_multiply_fusion.1
  68.9 1.3 fusion.60
  70.3 0.4 fusion.31
  70.7 0.1 fusion.55
  70.9 0.2 copy.92
  71.0 0.1 copy.100
  71.2 15.6 %fusion = f32[1,7,7,7,96]{4,0,3,2,1:T(1,128)S(1)} fusion(bf16[2,10,14,22,96]{4,0,3,2,1:T(2,128)(2,1)} %copy-done.1, bf16[4,8,16,1,96]{4,2,1,0,3:T(8,128)(2,1)S(1)} %bitcast.90), kind=kOutput, calls=%fused_computation.2 | convolution fusion | flops 33718272 | bytes 1412736 | tf_op jit(solution)/shard_map/conv_general_dilated | solution.py:127
  86.7 0.1 copy.98
  86.9 0.2 copy.121
  87.2 3.3 %collective-permute-start.6 = (bf16[2,3,8,16,96]{4,0,3,2,1:T(2,128)(2,1)S(1)}, bf16[2,3,8,16,96]{4,0,3,2,1:T(2,128)(2,1)S(1)}, u32[]{:S(2)}, u32[]{:S(2)}) collective-permute-start(bf16[2,3,8,16,96]{4,0,3,2,1:T(2,128)(2,1)S(1)} %copy.121), channel_id=1, source_target_pairs={{0,4},{4,8},{8,12},{1,5},{5,9},{9,13},{2,6},{6,10},{10,14},{3,7},{... | collective-permute-start | bytes 442376 | tf_op jit(solution)/shard_map/ppermute | solution.py:21
  90.5 0.2 copy.122
  90.7 1.3 collective-permute-start.7
  92.0 13.7 %fusion.26 = f32[1,7,7,7,96]{4,0,3,2,1:T(1,128)S(1)} fusion(f32[1,7,7,7,96]{4,0,3,2,1:T(1,128)S(1)} %fusion, bf16[2,10,14,22,96]{4,0,3,2,1:T(2,128)(2,1)S(1)} %copy-done.2, bf16[4,8,16,1,96]{4,2,1,0,3:T(8,128)(2,1)S(1)} %bitcast.89), kind=kOutput, calls=%fused_computation.33 | convolution fusion | flops 33784128 | bytes 1544448 | tf_op jit(solution)/shard_map/conv_general_dilated | solution.py:127
  105.7 1.1 convolution_multiply_fusion
  106.8 0.1 constant_dynamic-update-slice_fusion.5
  107.0 0.3 constant_dynamic-update-slice_fusion.4
  107.3 0.2 constant_dynamic-update-slice_fusion.3
  107.4 0.4 fusion.53
  107.8 1.3 collective-permute-start.8
  109.1 1.3 collective-permute-start.9
  110.4 0.7 copy.128
  111.1 0.2 convert_reduce_fusion
  111.4 2.5 %collective-permute-done.8 = bf16[2,10,3,16,96]{4,0,3,2,1:T(2,128)(2,1)S(1)} collective-permute-done((bf16[2,10,3,16,96]{4,0,3,2,1:T(2,128)(2,1)S(1)}, bf16[2,10,3,16,96]{4,0,3,2,1:T(2,128)(2,1)S(1)}, u32[]{:S(2)}, u32[]{:S(2)}) %collective-permute-start.8) | collective-permute-done | bytes 184352 | tf_op jit(solution)/shard_map/ppermute | solution.py:21
  113.8 3.8 %collective-permute-done.9 = bf16[2,10,3,16,96]{4,0,3,2,1:T(2,128)(2,1)S(1)} collective-permute-done((bf16[2,10,3,16,96]{4,0,3,2,1:T(2,128)(2,1)S(1)}, bf16[2,10,3,16,96]{4,0,3,2,1:T(2,128)(2,1)S(1)}, u32[]{:S(2)}, u32[]{:S(2)}) %collective-permute-start.9) | collective-permute-done | bytes 184352 | tf_op jit(solution)/shard_map/ppermute | solution.py:24
  117.7 0.7 pad_maximum_fusion.3
  118.4 1.3 collective-permute-start.10
  119.7 3.6 %collective-permute-start.11 = (bf16[2,10,14,3,96]{4,0,3,2,1:T(2,128)(2,1)S(1)}, bf16[2,10,14,3,96]{4,0,3,2,1:T(2,128)(2,1)S(1)}, u32[]{:S(2)}, u32[]{:S(2)}) collective-permute-start(bf16[2,10,14,3,96]{4,0,3,2,1:T(2,128)(2,1)S(1)} %get-tuple-element.52), channel_id=1, source_target_pairs={{1,0},{3,2},{5,4},{7,6},{9,8},{11,10},{13,12},{15,14},{17,16},{19,... | collective-permute-start | bytes 483848 | tf_op jit(solution)/shard_map/ppermute | solution.py:24
  123.4 28.9 %all-reduce = (f32[96]{0:T(128)}, f32[192]{0:T(256)}, f32[384]{0:T(512)}) all-reduce(f32[96]{0:T(128)S(1)} %broadcast_multiply_fusion.4, f32[192]{0:T(256)S(1)} %maximum_multiply_fusion, f32[384]{0:T(512)S(1)} %broadcast_multiply_fusion.3), channel_id=1, replica_groups=mesh['groups'=2,'depth'=4,'rows'=2,'cols'=2] {'depth','rows','cols'}, use_global_device_ids=true, to_apply=%region_6.0 | all-reduce | flops 672 | bytes 5376 | tf_op jit(solution)/shard_map/psum | solution.py:138
  152.3 52.6 %all-reduce.4.cloned.1.call-done = (f32[96,1,7,7,7]{0,4,3,2,1:T(8,128)}, f32[96,384]{1,0:T(8,128)}, f32[384,96]{0,1:T(8,128)}) async-done(((f32[96,1,7,7,7]{0,4,3,2,1:T(8,128)}, f32[96,384]{1,0:T(8,128)}, f32[384,96]{0,1:T(8,128)}), (f32[96,1,7,7,7]{0,4,3,2,1:T(8,128)}, f32[96,384]{1,0:T(8,128)}, f32[384,96]{0,1:T(8,128)})) %all-reduce.4.cloned.1.call-update) | async-done | bytes 426640 | tf_op jit(solution)/shard_map/psum | solution.py:138
  204.9 1.8 copy.102
  206.6 7.8 %fusion.81 = bf16[2,10,14,22,96]{4,0,3,2,1:T(2,128)(2,1)S(1)} fusion(bf16[2,10,14,3,96]{4,0,3,2,1:T(2,128)(2,1)S(1)} %collective-permute-done.11, bf16[2,10,3,16,96]{4,0,3,2,1:T(2,128)(2,1)S(1)} %collective-permute-done.9, bf16[2,10,8,16,96]{4,0,3,2,1:T(2,128)(2,1)S(1)} %constant_dynamic-update-slice_fusion.3, ...), kind=kLoop, calls=%fused_computation.8.clone.1 | loop fusion | flops 2365440 | bytes 2365440 | tf_op jit(solution)/shard_map/conv_general_dilated | solution.py:30
  214.5 20.6 %fusion.4 = f32[2,4,8,16,96]{4,0,3,2,1:T(2,128)S(1)} fusion(bf16[96,1,7,7,7]{0,4,3,2,1:T(8,128)(2,1)S(1)} %copy-done.11, bf16[2,10,14,22,96]{4,0,3,2,1:T(2,128)(2,1)S(1)} %fusion.81), kind=kOutput, calls=%fused_computation.7 | convolution fusion | flops 67436544 | bytes 1641792 | tf_op jit(solution)/shard_map/conv_general_dilated | solution.py:30
  235.2 0.9 reshape.68
  236.2 0.7 copy.136
  236.8 0.7 copy.137
  (49 shorter events, 0.6 us)
Async XLA Ops:
  7.2 18.2 %copy-start = (bf16[768,192]{0,1:T(8,128)(2,1)S(1)}, bf16[768,192]{0,1:T(8,128)(2,1)}, u32[]{:S(2)}) copy-start(bf16[768,192]{0,1:T(8,128)(2,1)} %param.15) | copy-start | bytes 884740
  7.2 7.1 %copy-start.3 = (bf16[2,4,8,1536]{3,2,1,0:T(8,128)(2,1)S(1)}, bf16[2,4,8,1536]{3,2,1,0:T(8,128)(2,1)}, u32[]{:S(2)}) copy-start(bf16[2,4,8,1536]{3,2,1,0:T(8,128)(2,1)} %param.11) | copy-start | bytes 589828
  7.2 7.6 %copy-start.7 = (bf16[768]{0:T(1024)(128)(2,1)S(1)}, bf16[768]{0:T(1024)(128)(2,1)}, u32[]{:S(2)}) copy-start(bf16[768]{0:T(1024)(128)(2,1)} %param.12) | copy-start | bytes 4612
  7.2 197.7 %all-reduce.4.cloned.1.call-start = ((), (), s32[]{:S(2)}) async-start(), calls=%async_computation | async-start | bytes 991232 | tf_op jit(solution)/shard_map/psum | solution.py:138
  8.8 7.6 %collective-permute-start = (bf16[2,3,8,16,96]{4,0,3,2,1:T(2,128)(2,1)S(1)}, bf16[2,3,8,16,96]{4,0,3,2,1:T(2,128)(2,1)S(1)}, u32[]{:S(2)}, u32[]{:S(2)}) collective-permute-start(bf16[2,3,8,16,96]{4,0,3,2,1:T(2,128)(2,1)S(1)} %copy.119), channel_id=1, source_target_pairs={{0,4},{4,8},{8,12},{1,5},{5,9},{9,13},{2,6},{6,10},{10,14},{3,7},{... | collective-permute-start | bytes 442376 | tf_op jit(solution)/shard_map/ppermute | solution.py:21
  13.0 7.4 %collective-permute-start.1 = (bf16[2,3,8,16,96]{4,0,3,2,1:T(2,128)(2,1)S(1)}, bf16[2,3,8,16,96]{4,0,3,2,1:T(2,128)(2,1)S(1)}, u32[]{:S(2)}, u32[]{:S(2)}) collective-permute-start(bf16[2,3,8,16,96]{4,0,3,2,1:T(2,128)(2,1)S(1)} %copy.120), channel_id=1, source_target_pairs={{4,0},{8,4},{12,8},{5,1},{9,5},{13,9},{6,2},{10,6},{14,10},{7,3},{... | collective-permute-start | bytes 442376 | tf_op jit(solution)/shard_map/ppermute | solution.py:24
  14.5 11.0 %copy-start.9 = (f32[192]{0:T(256)S(1)}, f32[192]{0:T(256)}, u32[]{:S(2)}) copy-start(f32[192]{0:T(256)} %param.16) | copy-start | bytes 2308
  20.9 6.6 %collective-permute-start.2 = (bf16[2,10,3,16,96]{4,0,3,2,1:T(2,128)(2,1)S(1)}, bf16[2,10,3,16,96]{4,0,3,2,1:T(2,128)(2,1)S(1)}, u32[]{:S(2)}, u32[]{:S(2)}) collective-permute-start(bf16[2,10,3,16,96]{4,0,3,2,1:T(2,128)(2,1)S(1)} %get-tuple-element.57), channel_id=1, source_target_pairs={{0,2},{1,3},{4,6},{5,7},{8,10},{9,11},{12,14},{13,15},{16,18},{17,... | collective-permute-start | bytes 552968 | tf_op jit(solution)/shard_map/ppermute | solution.py:21
  24.1 7.3 %collective-permute-start.3 = (bf16[2,10,3,16,96]{4,0,3,2,1:T(2,128)(2,1)S(1)}, bf16[2,10,3,16,96]{4,0,3,2,1:T(2,128)(2,1)S(1)}, u32[]{:S(2)}, u32[]{:S(2)}) collective-permute-start(bf16[2,10,3,16,96]{4,0,3,2,1:T(2,128)(2,1)S(1)} %get-tuple-element.58), channel_id=1, source_target_pairs={{2,0},{3,1},{6,4},{7,5},{10,8},{11,9},{14,12},{15,13},{18,16},{19,... | collective-permute-start | bytes 552968 | tf_op jit(solution)/shard_map/ppermute | solution.py:24
  32.1 6.5 %collective-permute-start.4 = (bf16[2,10,14,3,96]{4,0,3,2,1:T(2,128)(2,1)S(1)}, bf16[2,10,14,3,96]{4,0,3,2,1:T(2,128)(2,1)S(1)}, u32[]{:S(2)}, u32[]{:S(2)}) collective-permute-start(bf16[2,10,14,3,96]{4,0,3,2,1:T(2,128)(2,1)S(1)} %get-tuple-element.53), channel_id=1, source_target_pairs={{0,1},{2,3},{4,5},{6,7},{8,9},{10,11},{12,13},{14,15},{16,17},{18,... | collective-permute-start | bytes 483848 | tf_op jit(solution)/shard_map/ppermute | solution.py:21
  33.4 5.9 %collective-permute-start.5 = (bf16[2,10,14,3,96]{4,0,3,2,1:T(2,128)(2,1)S(1)}, bf16[2,10,14,3,96]{4,0,3,2,1:T(2,128)(2,1)S(1)}, u32[]{:S(2)}, u32[]{:S(2)}) collective-permute-start(bf16[2,10,14,3,96]{4,0,3,2,1:T(2,128)(2,1)S(1)} %get-tuple-element.54), channel_id=1, source_target_pairs={{1,0},{3,2},{5,4},{7,6},{9,8},{11,10},{13,12},{15,14},{17,16},{19,... | collective-permute-start | bytes 483848 | tf_op jit(solution)/shard_map/ppermute | solution.py:24
  38.6 8.5 %copy-start.10 = (bf16[96,1,7,7,7]{0,4,3,2,1:T(8,128)(2,1)S(1)}, bf16[96,1,7,7,7]{0,4,3,2,1:T(8,128)(2,1)}, u32[]{:S(2)}) copy-start(bf16[96,1,7,7,7]{0,4,3,2,1:T(8,128)(2,1)} %param.13) | copy-start | bytes 197572
  38.6 8.6 %copy-start.13 = (f32[96]{0:T(128)S(1)}, f32[96]{0:T(128)}, u32[]{:S(2)}) copy-start(f32[96]{0:T(128)} %param.14) | copy-start | bytes 1156
  47.1 19.1 %copy-start.1 = (bf16[2,10,14,22,96]{4,0,3,2,1:T(2,128)(2,1)}, bf16[2,10,14,22,96]{4,0,3,2,1:T(2,128)(2,1)S(1)}, u32[]{:S(2)}) copy-start(bf16[2,10,14,22,96]{4,0,3,2,1:T(2,128)(2,1)S(1)} %pad_maximum_fusion) | copy-start | bytes 3548164
  66.2 0.9 copy-start.4
  66.2 0.9 copy-start.8
  67.6 1.4 copy-start.12
  86.9 5.1 %copy-start.2 = (bf16[2,10,14,22,96]{4,0,3,2,1:T(2,128)(2,1)S(1)}, bf16[2,10,14,22,96]{4,0,3,2,1:T(2,128)(2,1)}, u32[]{:S(2)}) copy-start(bf16[2,10,14,22,96]{4,0,3,2,1:T(2,128)(2,1)} %copy-done.1) | copy-start | bytes 3548164
  87.2 19.7 %collective-permute-start.6 = (bf16[2,3,8,16,96]{4,0,3,2,1:T(2,128)(2,1)S(1)}, bf16[2,3,8,16,96]{4,0,3,2,1:T(2,128)(2,1)S(1)}, u32[]{:S(2)}, u32[]{:S(2)}) collective-permute-start(bf16[2,3,8,16,96]{4,0,3,2,1:T(2,128)(2,1)S(1)} %copy.121), channel_id=1, source_target_pairs={{0,4},{4,8},{8,12},{1,5},{5,9},{9,13},{2,6},{6,10},{10,14},{3,7},{... | collective-permute-start | bytes 442376 | tf_op jit(solution)/shard_map/ppermute | solution.py:21
  90.7 16.5 %collective-permute-start.7 = (bf16[2,3,8,16,96]{4,0,3,2,1:T(2,128)(2,1)S(1)}, bf16[2,3,8,16,96]{4,0,3,2,1:T(2,128)(2,1)S(1)}, u32[]{:S(2)}, u32[]{:S(2)}) collective-permute-start(bf16[2,3,8,16,96]{4,0,3,2,1:T(2,128)(2,1)S(1)} %copy.122), channel_id=1, source_target_pairs={{4,0},{8,4},{12,8},{5,1},{9,5},{13,9},{6,2},{10,6},{14,10},{7,3},{... | collective-permute-start | bytes 442376 | tf_op jit(solution)/shard_map/ppermute | solution.py:24
  107.8 6.1 %collective-permute-start.8 = (bf16[2,10,3,16,96]{4,0,3,2,1:T(2,128)(2,1)S(1)}, bf16[2,10,3,16,96]{4,0,3,2,1:T(2,128)(2,1)S(1)}, u32[]{:S(2)}, u32[]{:S(2)}) collective-permute-start(bf16[2,10,3,16,96]{4,0,3,2,1:T(2,128)(2,1)S(1)} %get-tuple-element.55), channel_id=1, source_target_pairs={{0,2},{1,3},{4,6},{5,7},{8,10},{9,11},{12,14},{13,15},{16,18},{17,... | collective-permute-start | bytes 552968 | tf_op jit(solution)/shard_map/ppermute | solution.py:21
  109.1 8.6 %collective-permute-start.9 = (bf16[2,10,3,16,96]{4,0,3,2,1:T(2,128)(2,1)S(1)}, bf16[2,10,3,16,96]{4,0,3,2,1:T(2,128)(2,1)S(1)}, u32[]{:S(2)}, u32[]{:S(2)}) collective-permute-start(bf16[2,10,3,16,96]{4,0,3,2,1:T(2,128)(2,1)S(1)} %get-tuple-element.56), channel_id=1, source_target_pairs={{2,0},{3,1},{6,4},{7,5},{10,8},{11,9},{14,12},{15,13},{18,16},{19,... | collective-permute-start | bytes 552968 | tf_op jit(solution)/shard_map/ppermute | solution.py:24
  118.4 88.2 %collective-permute-start.10 = (bf16[2,10,14,3,96]{4,0,3,2,1:T(2,128)(2,1)S(1)}, bf16[2,10,14,3,96]{4,0,3,2,1:T(2,128)(2,1)S(1)}, u32[]{:S(2)}, u32[]{:S(2)}) collective-permute-start(bf16[2,10,14,3,96]{4,0,3,2,1:T(2,128)(2,1)S(1)} %get-tuple-element.51), channel_id=1, source_target_pairs={{0,1},{2,3},{4,5},{6,7},{8,9},{10,11},{12,13},{14,15},{16,17},{18,... | collective-permute-start | bytes 483848 | tf_op jit(solution)/shard_map/ppermute | solution.py:21
  119.7 86.9 %collective-permute-start.11 = (bf16[2,10,14,3,96]{4,0,3,2,1:T(2,128)(2,1)S(1)}, bf16[2,10,14,3,96]{4,0,3,2,1:T(2,128)(2,1)S(1)}, u32[]{:S(2)}, u32[]{:S(2)}) collective-permute-start(bf16[2,10,14,3,96]{4,0,3,2,1:T(2,128)(2,1)S(1)} %get-tuple-element.52), channel_id=1, source_target_pairs={{1,0},{3,2},{5,4},{7,6},{9,8},{11,10},{13,12},{15,14},{17,16},{19,... | collective-permute-start | bytes 483848 | tf_op jit(solution)/shard_map/ppermute | solution.py:24
  206.6 7.8 %copy-start.11 = (bf16[96,1,7,7,7]{0,4,3,2,1:T(8,128)(2,1)S(1)}, bf16[96,1,7,7,7]{0,4,3,2,1:T(8,128)(2,1)}, u32[]{:S(2)}) copy-start(bf16[96,1,7,7,7]{0,4,3,2,1:T(8,128)(2,1)} %param.13) | copy-start | bytes 197572
  235.1 1.0 copy-start.6
  235.1 1.7 copy-start.5
Sparse Core Ops, SparseCore 0:
  111.3 93.5 all-reduce.3
where the time goes:
time: 249 us; the launch traced here: 245 us
  matrix products  73.7 us (30%)
  waiting for transfers between devices  70.7 us (28%)
  blocking collectives  28.9 us (12%)
  starting transfers between devices  28.3 us (11%)
  other arithmetic  17.7 us (7%)
  between operations  15 us (6%)
  local copies, waits for them, and re-layouts  10.4 us (4%)
    psum x1, waiting for transfers between devices, local(): summed_conv = lax.psum((term_kernel, term_bias), ('depth', 'rows', 'cols'))  52.6 us
    conv_general_dilated x2, matrix products, depthwise(): lax.conv_general_dilated(padded, kernel, (1, 1, 1), 'VALID', dimension_nu...  39.7 us
    conv_general_dilated x2, matrix products, local(): lax.conv_general_dilated(padded[crop_index][None], slope_vol[crop_index][...  29.3 us
    psum x1, blocking collectives, local(): summed_conv = lax.psum((term_kernel, term_bias), ('depth', 'rows', 'cols'))  28.9 us
    ppermute x6, starting transfers between devices, padded_2(): lax.ppermute(lax.slice_in_dim(block, block.shape[dim] - width, None, axis...  14.4 us
    ppermute x6, starting transfers between devices, padded_2(): lax.ppermute(lax.slice_in_dim(block, 0, width, axis=dim), axis, backward)  13.9 us
    ppermute x6, waiting for transfers between devices, padded_2(): lax.ppermute(lax.slice_in_dim(block, 0, width, axis=dim), axis, backward)  12.1 us
    conv_general_dilated x1, other arithmetic, depthwise(): lax.conv_general_dilated(padded, kernel, (1, 1, 1), 'VALID', dimension_nu...  7.79 us
  transfers between devices with their start and end apart: 13, of which 8 were waited for; matrix products, arithmetic and copies ran while one was open for 8% of the time, Pallas kernels for 0%

commit v1 on v0

v1 whole, which is shorter than its diff:
```python
import functools
import math

import jax
import jax.numpy as jnp
from jax import lax
from jax.experimental import pallas as pl
from jax.experimental.pallas import tpu as pltpu
from jax.sharding import PartitionSpec as P

K = 7
HALF = K // 2
LANES = 128
SUB = 8
TAPS = K * K * K
EPSILON = 1e-06
MESH = pl.DeviceIdType.MESH
GELU_C = math.sqrt(2.0 / math.pi)
DIRS = tuple((dz, dx) for dz in (-1, 0, 1) for dx in (-1, 0, 1) if (dz, dx) != (0, 0))


def both(*conds):
    out = conds[0]
    for cond in conds[1:]:
        out = jnp.logical_and(out, cond)
    return out


def source_cells(step, extent):
    return {-1: slice(0, HALF), 0: slice(0, extent), 1: slice(extent - HALF, extent)}[step]


def target_cells(step, extent):
    return {
        -1: slice(HALF + extent, 2 * HALF + extent),
        0: slice(HALF, HALF + extent),
        1: slice(0, HALF),
    }[step]


class Halo:
    def __init__(self, own, pad, sems, where, counts):
        self.own, self.pad = own, pad
        self.send, self.recv, self.col_send, self.col_recv = sems
        self.grp, self.z, self.x, self.c = where
        self.nz, self.nx, self.nc = counts
        self.extents = own.shape[1], own.shape[2], own.shape[3]

    def inside(self, dz, dx, dc):
        z, x, c = self.z + dz, self.x + dx, self.c + dc
        return both(z >= 0, z < self.nz, x >= 0, x < self.nx, c >= 0, c < self.nc)

    def plane(self, idx):
        dz, dx = DIRS[idx]
        depth, rows, tiles = self.extents
        return pltpu.make_async_remote_copy(
            src_ref=self.own.at[:, source_cells(dz, depth), source_cells(dx, rows)],
            dst_ref=self.pad.at[
                :, target_cells(dz, depth), target_cells(dx, rows), slice(1, tiles + 1)
            ],
            send_sem=self.send.at[idx],
            recv_sem=self.recv.at[idx],
            device_id=(self.grp, self.z + dz, self.x + dx, self.c),
            device_id_type=MESH,
        )

    def column(self, idx, side):
        dc = (-1, 1)[side]
        depth, rows, tiles = self.extents
        dst_tile = tiles + 1 if dc < 0 else 0
        if idx == len(DIRS):
            area = (slice(None), target_cells(0, depth), target_cells(0, rows))
            src = self.own.at[:, :, :, 0 if dc < 0 else tiles - 1]
        else:
            dz, dx = DIRS[idx]
            area = (slice(None), target_cells(dz, depth), target_cells(dx, rows))
            src = self.pad.at[area + (1 if dc < 0 else tiles,)]
        return pltpu.make_async_remote_copy(
            src_ref=src,
            dst_ref=self.pad.at[area + (dst_tile,)],
            send_sem=self.col_send.at[side, idx],
            recv_sem=self.col_recv.at[side, idx],
            device_id=(self.grp, self.z, self.x, self.c + dc),
            device_id_type=MESH,
        )

    def fill_edges(self):
        pad = self.pad
        depth, rows, tiles = self.extents

        def clear(cond, area):
            @pl.when(cond)
            def _():
                view = pad.at[area]
                view[...] = jnp.zeros(view.shape, view.dtype)

        every = slice(None)
        clear(self.z == 0, (every, slice(0, HALF)))
        clear(self.z == self.nz - 1, (every, slice(HALF + depth, 2 * HALF + depth)))
        clear(self.x == 0, (every, every, slice(0, HALF)))
        clear(self.x == self.nx - 1, (every, every, slice(HALF + rows, 2 * HALF + rows)))
        clear(self.c == 0, (every, every, every, slice(0, 1)))
        clear(self.c == self.nc - 1, (every, every, every, slice(tiles + 1, tiles + 2)))

    def start(self):
        for idx, (dz, dx) in enumerate(DIRS):
            @pl.when(self.inside(dz, dx, 0))
            def _():
                self.plane(idx).start()
        for side in range(2):
            @pl.when(self.inside(0, 0, (-1, 1)[side]))
            def _():
                self.column(len(DIRS), side).start()

    def centre(self):
        depth, rows, tiles = self.extents
        self.pad[:, HALF : HALF + depth, HALF : HALF + rows, 1 : tiles + 1] = self.own[...]

    def relay(self):
        for idx, (dz, dx) in enumerate(DIRS):
            @pl.when(self.inside(-dz, -dx, 0))
            def _():
                self.plane(idx).wait_recv()
                for side in range(2):
                    @pl.when(self.inside(-dz, -dx, (-1, 1)[side]))
                    def _():
                        self.column(idx, side).start()

    def finish(self):
        for idx, (dz, dx) in enumerate(DIRS + ((0, 0),)):
            for side in range(2):
                dc = (-1, 1)[side]

                @pl.when(self.inside(-dz, -dx, -dc))
                def _():
                    self.column(idx, side).wait_recv()

                @pl.when(self.inside(-dz, -dx, dc))
                def _():
                    self.column(idx, side).wait_send()

        for idx, (dz, dx) in enumerate(DIRS):
            @pl.when(self.inside(dz, dx, 0))
            def _():
                self.plane(idx).wait_send()


def widen(pad, wide):
    crops, depth = pad.shape[0], pad.shape[1]
    tiles = pad.shape[3]

    def one(step, _):
        crop, d = step // depth, step % depth
        for tile in range(tiles):
            wide[crop, d, :, tile * SUB : (tile + 1) * SUB, :] = pad[crop, d, :, tile].astype(
                jnp.float32
            )
        return 0

    lax.fori_loop(0, crops * depth, one, 0)


def conv_tile(wide, taps, crop, tile, extents, flip):
    depth, rows = extents[0], extents[1]

    def row_tap(j, accs):
        accs = list(accs)
        for k in range(K):
            jw, kw = (K - 1 - j, K - 1 - k) if flip else (j, k)
            weights = [taps[jw, kw, K - 1 - i if flip else i] for i in range(K)]
            start = (tile + 1) * SUB - HALF + k
            for h in range(rows):
                cells = [wide[crop, d, j + h, start : start + SUB, :] for d in range(depth + K - 1)]
                for d in range(depth):
                    acc = accs[d * rows + h]
                    for i in range(K):
                        acc = acc + cells[d + i] * weights[i]
                    accs[d * rows + h] = acc
        return tuple(accs)

    zero = jnp.zeros((SUB, LANES), jnp.float32)
    return lax.fori_loop(0, K, row_tap, (zero,) * (depth * rows))


def kernel(
    counts, channels, row_of,
    x_ref, g_ref, taps_ref, vec_ref, inw_ref, inb_ref, outw_ref,
    gi_ref, red_ref,
    xp, sp, so, wide, conv_s, slope_s, accw, accb, accf, part, part_low, inbox, mine, full,
    halo_sems_0, halo_sems_1, halo_sems_2, halo_sems_3,
    slope_sems_0, slope_sems_1, slope_sems_2, slope_sems_3,
    rs_send, rs_recv, ag_send, ag_recv,
):
    nz, nx, nc = counts
    total = nz * nx * nc
    grp, z, x, c = (lax.axis_index(name) for name in ("groups", "depth", "rows", "cols"))
    me = (z * nx + x) * nc + c
    crops, depth, rows, tiles = x_ref.shape[:4]
    extents = (depth, rows, tiles)
    voxels = depth * rows * SUB
    hidden = inw_ref.shape[1]
    chunk = part.shape[0] // total

    def peer(offset):
        other = lax.rem(me + offset, total)
        return other, (grp, other // (nx * nc), (other // nc) % nx, other % nc)

    barrier = pltpu.get_barrier_semaphore()

    def greet(offset, _):
        pl.semaphore_signal(barrier, inc=1, device_id=peer(offset)[1], device_id_type=MESH)
        return 0

    lax.fori_loop(1, total, greet, 0)
    where = (grp, z, x, c)
    halo_x = Halo(x_ref, xp, (halo_sems_0, halo_sems_1, halo_sems_2, halo_sems_3), where, counts)
    halo_s = Halo(so, sp, (slope_sems_0, slope_sems_1, slope_sems_2, slope_sems_3), where, counts)
    pl.semaphore_wait(barrier, total - 1)
    halo_x.start()
    halo_x.fill_edges()
    halo_x.centre()
    halo_s.fill_edges()
    accw[...] = jnp.zeros_like(accw)
    accb[...] = jnp.zeros_like(accb)
    accf[...] = jnp.zeros_like(accf)
    tail = row_of["end"] // SUB * SUB
    part[tail:, :] = jnp.zeros((part.shape[0] - tail, LANES), jnp.float32)
    halo_x.relay()
    halo_x.finish()
    widen(xp, wide)

    def forward(crop, _):
        for tile in range(tiles):
            accs = conv_tile(wide, taps_ref, crop, tile, extents, False)
            for d in range(depth):
                for h in range(rows):
                    conv_s[crop * tiles + tile, d, h] = accs[d * rows + h]
        return 0

    lax.fori_loop(0, crops, forward, 0)

    conv_bias, scale, shift = vec_ref[0:1, :], vec_ref[1:2, :], vec_ref[2:3, :]
    real = lax.broadcasted_iota(jnp.int32, (1, LANES), 1) < channels

    def mlp(step, _):
        crop, tile = step // tiles, step % tiles
        conv = conv_s[step].reshape(voxels, LANES) + conv_bias
        mean = jnp.sum(conv, axis=1, keepdims=True) * (1.0 / channels)
        centred = jnp.where(real, conv - mean, 0.0)
        variance = jnp.sum(centred * centred, axis=1, keepdims=True) * (1.0 / channels)
        inverse = lax.rsqrt(variance + EPSILON)
        normed = centred * inverse
        hidden_in = (normed * scale + shift).astype(jnp.bfloat16)
        grad = g_ref[crop, :, :, tile].astype(jnp.float32).reshape(voxels, LANES)
        grad = grad.astype(jnp.bfloat16)
        pre = jnp.dot(hidden_in, inw_ref[...], preferred_element_type=jnp.float32) + inb_ref[...]
        square = pre * pre
        th = jnp.tanh(GELU_C * (pre + 0.044715 * (square * pre)))
        act_low = (0.5 * pre * (1.0 + th)).astype(jnp.bfloat16)
        slope_act = 0.5 * (1.0 + th) + 0.5 * pre * (1.0 - th * th) * (
            GELU_C * (1.0 + (3.0 * 0.044715) * square)
        )
        grad_act = lax.dot_general(
            grad, outw_ref[...], (((1,), (1,)), ((), ())), preferred_element_type=jnp.float32
        )
        grad_pre = grad_act * slope_act
        grad_low = grad_pre.astype(jnp.bfloat16)
        grad_hidden = lax.dot_general(
            grad_low, inw_ref[...], (((1,), (1,)), ((), ())), preferred_element_type=jnp.float32
        )
        over_voxels = (((0,), (0,)), ((), ()))
        accw[0] += lax.dot_general(
            hidden_in, grad_low, over_voxels, preferred_element_type=jnp.float32
        )
        accw[1] += lax.dot_general(grad, act_low, over_voxels, preferred_element_type=jnp.float32)
        accb[0:1, :] += jnp.sum(grad_pre, axis=0, keepdims=True)
        accf[1:2, :] += jnp.sum(grad_hidden * normed, axis=0, keepdims=True)
        accf[2:3, :] += jnp.sum(grad_hidden, axis=0, keepdims=True)
        grad_normed = grad_hidden * scale
        mean_g = jnp.sum(grad_normed, axis=1, keepdims=True) * (1.0 / channels)
        mean_gn = jnp.sum(grad_normed * normed, axis=1, keepdims=True) * (1.0 / channels)
        slope = (grad_normed - mean_g - normed * mean_gn) * inverse
        slope = slope.astype(jnp.bfloat16).astype(jnp.float32)
        accf[0:1, :] += jnp.sum(slope, axis=0, keepdims=True)
        slope = slope.reshape(depth, rows, SUB, LANES)
        slope_s[step] = slope
        so[crop, :, :, tile] = slope.astype(jnp.bfloat16)
        return 0

    lax.fori_loop(0, crops * tiles, mlp, 0)
    halo_s.start()
    halo_s.centre()

    def kernel_grad(j, _):
        for k in range(K):
            def gather(crop, accs):
                accs = list(accs)
                for tile in range(tiles):
                    start = (tile + 1) * SUB - HALF + k
                    for h in range(rows):
                        cells = [
                            wide[crop, d, j + h, start : start + SUB, :]
                            for d in range(depth + K - 1)
                        ]
                        for d in range(depth):
                            slope = slope_s[crop * tiles + tile, d, h]
                            for i in range(K):
                                accs[i] = accs[i] + cells[d + i] * slope
                return tuple(accs)

            zero = jnp.zeros((SUB, LANES), jnp.float32)
            accs = lax.fori_loop(0, crops, gather, (zero,) * K)
            for i in range(K):
                row = row_of["kernel"] + (i * K + j) * K + k
                part[pl.ds(row, 1), :] = jnp.sum(accs[i], axis=0, keepdims=True)
        return 0

    lax.fori_loop(0, K, kernel_grad, 0)
    halo_s.relay()

    for which, name in enumerate(("in", "out")):
        for block in range(hidden // LANES):
            first = row_of[name] + block * channels
            part[first : first + channels, :] = accw[
                which, 0:channels, block * LANES : (block + 1) * LANES
            ]
    part[row_of["small"] : row_of["small"] + 3, :] = accf[0:3, :]
    for block in range(hidden // LANES):
        row = row_of["in_bias"] + block
        part[row : row + 1, :] = accb[0:1, block * LANES : (block + 1) * LANES]
    part_low[...] = part[...].astype(jnp.bfloat16)

    def scatter(offset):
        other, device = peer(offset)
        return pltpu.make_async_remote_copy(
            src_ref=part_low.at[pl.ds(pl.multiple_of(other * chunk, chunk), chunk)],
            dst_ref=inbox.at[offset],
            send_sem=rs_send.at[offset],
            recv_sem=rs_recv.at[offset],
            device_id=device,
            device_id_type=MESH,
        )

    my_rows = pl.ds(pl.multiple_of(me * chunk, chunk), chunk)

    def spread(offset):
        return pltpu.make_async_remote_copy(
            src_ref=mine,
            dst_ref=full.at[my_rows],
            send_sem=ag_send.at[offset],
            recv_sem=ag_recv.at[offset],
            device_id=peer(offset)[1],
            device_id_type=MESH,
        )

    def arrived(offset):
        origin = lax.rem(me + total - offset, total)
        return pltpu.make_async_remote_copy(
            src_ref=mine,
            dst_ref=full.at[pl.ds(pl.multiple_of(origin * chunk, chunk), chunk)],
            send_sem=ag_send.at[offset],
            recv_sem=ag_recv.at[offset],
            device_id=peer(offset)[1],
            device_id_type=MESH,
        )

    def each(fn):
        def step(offset, _):
            fn(offset)
            return 0

        lax.fori_loop(1, total, step, 0)

    each(lambda offset: scatter(offset).start())
    halo_s.finish()
    widen(sp, wide)

    def backward(crop):
        for tile in range(tiles):
            accs = conv_tile(wide, taps_ref, crop, tile, extents, True)
            for d in range(depth):
                for h in range(rows):
                    grad = g_ref[crop, d, h, tile].astype(jnp.float32)
                    gi_ref[crop, d, h, tile] = (grad + accs[d * rows + h]).astype(jnp.bfloat16)

    def backward_loop(first, last):
        def step(crop, _):
            backward(crop)
            return 0

        lax.fori_loop(first, last, step, 0)

    backward_loop(0, crops // 2)

    each(lambda offset: scatter(offset).wait())

    def add(offset, acc):
        return acc + inbox[offset].astype(jnp.float32)

    summed = lax.fori_loop(1, total, add, part[my_rows, :])
    mine[...] = summed.astype(jnp.bfloat16)
    full[my_rows, :] = mine[...]
    each(lambda offset: spread(offset).start())
    backward_loop(crops // 2, crops)

    def settle(offset):
        spread(offset).wait_send()
        arrived(offset).wait_recv()

    each(settle)
    red_ref[...] = full[...].astype(jnp.float32)


def local(
    counts, volume, grad_out, report, conv_kernel, conv_bias,
    film_weight, film_bias, in_weight, in_bias, out_weight,
):
    crops, slices, lines, merged = volume.shape
    channels = conv_kernel.shape[0]
    hidden = in_weight.shape[1]
    width = merged // channels
    tiles = width // SUB
    extra = LANES - channels
    block = (crops, slices, lines, tiles, SUB, LANES)

    def to_block(array):
        array = array.reshape(crops, slices, lines, tiles, SUB, channels)
        return jnp.pad(array, ((0, 0),) * 5 + ((0, extra),))

    film = jnp.dot(report[None, :], film_weight, preferred_element_type=jnp.float32)[0] + film_bias
    vecs = jnp.stack([conv_bias, 1.0 + film[:channels], film[channels:]])
    vecs = jnp.pad(vecs, ((0, SUB - 3), (0, extra)))
    taps = jnp.transpose(conv_kernel[:, 0].astype(jnp.float32), (2, 3, 1, 0))
    taps = jnp.broadcast_to(
        jnp.pad(taps, ((0, 0),) * 3 + ((0, extra),))[:, :, :, None, :], (K, K, K, SUB, LANES)
    )
    total = counts[0] * counts[1] * counts[2]
    blocks = hidden // LANES
    row_of = {"in": 0, "out": blocks * channels, "kernel": 2 * blocks * channels}
    row_of["small"] = row_of["kernel"] + TAPS
    row_of["in_bias"] = row_of["small"] + 3
    row_of["end"] = row_of["in_bias"] + blocks
    unit = 16 * total
    all_rows = -(-row_of["end"] // unit) * unit
    chunk = all_rows // total
    padded = (crops, slices + 2 * HALF, lines + 2 * HALF, tiles + 2, SUB, LANES)
    bf, f32 = jnp.bfloat16, jnp.float32
    dma = pltpu.SemaphoreType.DMA
    halo_sems = [dma((len(DIRS),))] * 2 + [dma((2, len(DIRS) + 1))] * 2
    grad_input, red = pl.pallas_call(
        functools.partial(kernel, counts, channels, row_of),
        out_shape=(
            jax.ShapeDtypeStruct(block, bf),
            jax.ShapeDtypeStruct((all_rows, LANES), f32),
        ),
        in_specs=[pl.BlockSpec(memory_space=pltpu.VMEM)] * 7,
        out_specs=(pl.BlockSpec(memory_space=pltpu.VMEM),) * 2,
        scratch_shapes=[
            pltpu.VMEM(padded, bf),
            pltpu.VMEM(padded, bf),
            pltpu.VMEM(block, bf),
            pltpu.VMEM(padded[:3] + (padded[3] * SUB, LANES), f32),
            pltpu.VMEM((crops * tiles, slices, lines, SUB, LANES), f32),
            pltpu.VMEM((crops * tiles, slices, lines, SUB, LANES), f32),
            pltpu.VMEM((2, LANES, hidden), f32),
            pltpu.VMEM((SUB, hidden), f32),
            pltpu.VMEM((SUB, LANES), f32),
            pltpu.VMEM((all_rows, LANES), f32),
            pltpu.VMEM((all_rows, LANES), bf),
            pltpu.VMEM((total, chunk, LANES), bf),
            pltpu.VMEM((chunk, LANES), bf),
            pltpu.VMEM((all_rows, LANES), bf),
        ]
        + halo_sems
        + halo_sems
        + [dma((total,))] * 4,
        compiler_params=pltpu.CompilerParams(
            collective_id=0, has_side_effects=True, vmem_limit_bytes=56 * 1024 * 1024
        ),
        name="block",
    )(
        to_block(volume),
        to_block(grad_out),
        taps,
        vecs,
        jnp.pad(in_weight, ((0, extra), (0, 0))),
        in_bias[None, :],
        jnp.pad(out_weight, ((0, 0), (0, extra))),
    )
    grad_input = grad_input[..., :channels].reshape(volume.shape)
    factor = 1.0 / math.sqrt(crops * slices * lines * width * total)
    red = red * factor

    def matrix(name):
        rows = red[row_of[name] : row_of[name] + blocks * channels, :]
        return rows.reshape(blocks, channels, LANES)

    grad_in_w = jnp.transpose(matrix("in"), (1, 0, 2)).reshape(channels, hidden)
    grad_out_w = jnp.transpose(matrix("out")[:, :, :], (0, 2, 1)).reshape(hidden, channels)
    grad_kernel = red[row_of["kernel"] : row_of["kernel"] + TAPS, :channels].T
    grad_kernel = grad_kernel.reshape(channels, 1, K, K, K)
    small = red[row_of["small"] : row_of["small"] + 3, :channels]
    grad_film = jnp.concatenate([small[1], small[2]])
    grad_in_b = red[row_of["in_bias"] : row_of["in_bias"] + blocks, :].reshape(hidden)
    return grad_input, grad_kernel, small[0], grad_film, grad_in_w, grad_in_b, grad_out_w


def solution(mesh):
    split = P("groups", "depth", "rows", "cols")
    in_specs = (split, split, P("groups")) + (P(),) * 7
    out_specs = (
        split,
        P("groups", None, None, None, None),
        P("groups"),
        P("groups"),
        P("groups", None),
        P("groups"),
        P("groups", None),
    )
    counts = tuple(mesh.shape[name] for name in ("depth", "rows", "cols"))
    return jax.shard_map(
        functools.partial(local, counts),
        mesh=mesh,
        in_specs=in_specs,
        out_specs=out_specs,
        check_vma=False,
    )
```

time: 249 us -> 81.6 us (0.33); the launches traced: 245 us -> 81.2 us
  matrix products: 73.7 us -> 0.13 us
  waiting for transfers between devices: 70.7 us -> 0 us
  Pallas kernels: 0 us -> 62.4 us
  blocking collectives: 28.9 us -> 0 us
  starting transfers between devices: 28.3 us -> 0 us
  between operations: 15 us -> 0.74 us
  other arithmetic: 17.7 us -> 4.72 us
  local copies, waits for them, and re-layouts: 10.4 us -> 13.3 us
    conv_general_dilated x4 -> x0, matrix products: 69 us -> none  [the longest x2 39.7 us: depthwise(): lax.conv_general_dilated(padded, kernel, (1, 1, 1), 'VALID', dimension_nu...]
    pallas_call x0 -> x1, Pallas kernels: none -> 62.4 us  [local(): pl.pallas_call(functools.partial(kernel, counts, channels, row_of), out_s...]
    psum x1 -> x0, waiting for transfers between devices: 52.6 us -> none  [local(): summed_conv = lax.psum((term_kernel, term_bias), ('depth', 'rows', 'cols'))]
    psum x1 -> x0, blocking collectives: 28.9 us -> none  [local(): summed_conv = lax.psum((term_kernel, term_bias), ('depth', 'rows', 'cols'))]
    ppermute x12 -> x0, starting transfers between devices: 28.2 us -> none  [the longest x6 14.4 us: padded_2(): lax.ppermute(lax.slice_in_dim(block, block.shape[dim] - width, None, axis...]
    ppermute x12 -> x0, waiting for transfers between devices: 18.1 us -> none  [the longest x6 12.1 us: padded_2(): lax.ppermute(lax.slice_in_dim(block, 0, width, axis=dim), axis, backward)]
    conv_general_dilated x1 -> x0, other arithmetic: 7.79 us -> none  [depthwise(): lax.conv_general_dilated(padded, kernel, (1, 1, 1), 'VALID', dimension_nu...]
    concatenate x1, other arithmetic: 7.76 us -> 0.64 us  [local(): grad_film = jnp.concatenate([small[1], small[2]])]
  transfers between devices with their start and end apart: 13 -> 0, of which waited for: 8 -> 0; matrix products, arithmetic and copies ran while one was open for 8% -> 0% of each run, Pallas kernels for 0% -> 0%
where the time goes in v1:
time: 81.6 us; the launch traced here: 81.2 us
  Pallas kernels  62.4 us (76%)
  local copies, waits for them, and re-layouts  13.3 us (16%)
  other arithmetic  4.72 us (6%)
    pallas_call x1, Pallas kernels, local(): pl.pallas_call(functools.partial(kernel, counts, channels, row_of), out_s...  62.4 us
    reshape x1, local copies, waits for them, and re-layouts, local(): grad_input = grad_input[..., :channels].reshape(volume.shape)  1.9 us
    unnamed x8, local copies, waits for them, and re-layouts  1.7 us

profile of v1, /device:TPU:1, one launch (start us, length us, event | category | flops | bytes accessed | tf_op | source)
XLA Modules:
  0.0 81.2 jit_solution(13890599737146763552)
XLA Ops:
  0.6 0.0 copy-start
  0.6 0.0 copy-start.2
  0.7 0.0 copy-start.1
  0.7 1.3 %broadcast_in_dim.5.inb_ref = f32[1,384]{1,0:T(1,128)} reshape(f32[384]{0:T(512)} %param.18) | data formatting | bytes 3072 | tf_op jit(solution)/shard_map/broadcast_in_dim | solution.py:487
  2.0 0.7 reshape.57
  2.7 0.0 copy-done
  2.7 0.1 fusion.1
  2.8 0.8 add.21
  3.6 0.1 add_bitcast_fusion
  3.6 1.3 %select_maximum_fusion.vec_ref = f32[8,128]{1,0:T(8,128)} fusion(f32[1,96]{1,0:T(1,128)S(1)} %get-tuple-element.31, f32[1,96]{1,0:T(1,128)S(1)} %get-tuple-element.30, f32[1,96]{1,0:T(1,128)} %bitcast.49), kind=kLoop, calls=%fused_computation.5 | loop fusion | flops 11264 | bytes 5248 | tf_op jit(solution)/shard_map/stack | solution.py:431
  4.9 1.5 %pad.31.inw_ref = bf16[128,384]{1,0:T(8,128)(2,1)} pad(bf16[96,384]{1,0:T(8,128)(2,1)} %param.17, bf16[]{:T(256)} %constant.6.clone.1), padding=0_32x0_0 | pad | bytes 172034 | tf_op jit(solution)/shard_map/jit(_pad)/pad | solution.py:486
  6.4 1.0 %copy.23 = bf16[384,96]{1,0:T(8,128)(2,1)S(1)} copy(bf16[384,96]{0,1:T(8,128)(2,1)} %param.19) | data formatting | bytes 147456 | tf_op args[9]
  7.4 0.7 pad.32.outw_ref
  8.1 0.9 %pad_convert_fusion = f32[7,7,7,128]{3,1,0,2:T(8,128)S(1)} fusion(bf16[7,7,7,96]{3,1,0,2:T(8,128)(2,1)} %bitcast.47), kind=kLoop, calls=%fused_computation.4 | loop fusion | flops 43904 | bytes 241472 | tf_op jit(solution)/shard_map/jit(_pad)/pad | solution.py:435
  9.1 0.0 copy-done.1
  9.1 0.2 reshape.48
  9.3 0.8 pad.26.x_ref
  10.1 0.0 copy-done.2
  10.1 0.2 reshape.49
  10.3 0.8 pad.27.g_ref
  11.1 1.2 %broadcast_in_dim.4.taps_ref = f32[7,7,7,8,128]{4,3,2,1,0:T(8,128)} broadcast(f32[7,7,7,128]{3,2,1,0:T(8,128)S(1)} %copy.22), dimensions={0,1,2,4} | broadcast | bytes 1580544 | tf_op jit(solution)/shard_map/broadcast_in_dim | solution.py:434
  12.3 62.4 %block.1 = (bf16[2,4,8,2,8,128]{5,4,3,2,1,0:T(8,128)(2,1)}, f32[1024,128]{1,0:T(8,128)}) custom-call(bf16[2,4,8,2,8,128]{5,4,3,2,1,0:T(8,128)(2,1)} %pad.26.x_ref, bf16[2,4,8,2,8,128]{5,4,3,2,1,0:T(8,128)(2,1)} %pad.27.g_ref, f32[7,7,7,8,128]{4,3,2,1,0:T(8,128)} %broadcast_in_dim.4.taps_ref, f32[8,128]{1,0:T(8,128)} %select_maximum_fusion.vec_ref, ...), custom_call_target="tpu_custom_call" | custom-call | tf_op jit(solution)/shard_map/block/pallas_call | solution.py:450
  74.7 1.9 %reshape.50 = bf16[2,4,8,1536]{3,2,1,0:T(8,128)(2,1)} reshape(bf16[2,4,8,2,8,96]{5,4,3,2,1,0:T(8,128)(2,1)} %bitcast.46) | data formatting | bytes 393216 | tf_op jit(solution)/shard_map/reshape | solution.py:490
  76.6 1.1 %broadcast_multiply_fusion = f32[1024,128]{1,0:T(8,128)S(1)} fusion(f32[1024,128]{1,0:T(8,128)} %get-tuple-element.10), kind=kLoop, calls=%fused_computation | loop fusion | flops 131072 | bytes 1048576 | tf_op jit(solution)/shard_map/mul | solution.py:492
  77.7 0.5 slice_bitcast_fusion.3
  78.2 0.6 pad_maximum_fusion
  78.8 0.6 slice_bitcast_fusion.1
  79.4 0.8 %reshape.59 = f32[96,1,7,7,7]{0,1,4,3,2:T(1,128)} reshape(f32[96,343]{0,1:T(8,128)S(1)} %slice_bitcast_fusion) | data formatting | bytes 263424 | tf_op jit(solution)/shard_map/reshape | solution.py:501
  80.3 0.1 copy.24
  80.4 0.1 copy.25
  80.5 0.7 copy_bitcast_fusion
  (3 shorter events, 0.1 us)
Async XLA Ops:
  0.6 2.0 %copy-start = (bf16[768,192]{0,1:T(8,128)(2,1)S(1)}, bf16[768,192]{0,1:T(8,128)(2,1)}, u32[]{:S(2)}) copy-start(bf16[768,192]{0,1:T(8,128)(2,1)} %param.15) | copy-start | bytes 884740
  0.6 9.5 %copy-start.2 = (bf16[2,4,8,1536]{3,2,1,0:T(8,128)(2,1)S(1)}, bf16[2,4,8,1536]{3,2,1,0:T(8,128)(2,1)}, u32[]{:S(2)}) copy-start(bf16[2,4,8,1536]{3,2,1,0:T(8,128)(2,1)} %param.11) | copy-start | bytes 589828
  0.7 8.4 %copy-start.1 = (bf16[2,4,8,1536]{3,2,1,0:T(8,128)(2,1)S(1)}, bf16[2,4,8,1536]{3,2,1,0:T(8,128)(2,1)}, u32[]{:S(2)}) copy-start(bf16[2,4,8,1536]{3,2,1,0:T(8,128)(2,1)} %param.10) | copy-start | bytes 589828

commit v2 on v1

--- a/solution.py
+++ b/solution.py
@@ -184,9 +184,9 @@
 
 def kernel(
     counts, channels, row_of,
-    x_ref, g_ref, taps_ref, vec_ref, inw_ref, inb_ref, outw_ref,
-    gi_ref, red_ref,
-    xp, sp, so, wide, conv_s, slope_s, accw, accb, accf, part, part_low, inbox, mine, full,
+    factor, x_raw, g_raw, kernel_ref, bias_ref, report_ref, fw_ref, small_ref, inw_raw, outw_raw,
+    gi_ref, gk_ref, gb_ref, gsmall_ref, ginw_ref, goutw_ref,
+    x_ref, g_ref, taps_ref, inw_ref, outw_ref, red_ref, xp, sp, so, wide, conv_s, slope_s, vec_ref, accw, accb, accf, part, part_low, inbox, mine, full,
     halo_sems_0, halo_sems_1, halo_sems_2, halo_sems_3,
     slope_sems_0, slope_sems_1, slope_sems_2, slope_sems_3,
     rs_send, rs_recv, ag_send, ag_recv,
@@ -195,10 +195,10 @@
     total = nz * nx * nc
     grp, z, x, c = (lax.axis_index(name) for name in ("groups", "depth", "rows", "cols"))
     me = (z * nx + x) * nc + c
-    crops, depth, rows, tiles = x_ref.shape[:4]
+    crops, depth, rows, tiles = x_raw.shape[:4]
     extents = (depth, rows, tiles)
     voxels = depth * rows * SUB
-    hidden = inw_ref.shape[1]
+    hidden = inw_raw.shape[1]
     chunk = part.shape[0] // total
 
     def peer(offset):
@@ -212,6 +212,9 @@
         return 0
 
     lax.fori_loop(1, total, greet, 0)
+    spare = LANES - channels
+    x_ref[..., 0:channels] = x_raw[...]
+    x_ref[..., channels:] = jnp.zeros(x_ref.shape[:-1] + (spare,), jnp.bfloat16)
     where = (grp, z, x, c)
     halo_x = Halo(x_ref, xp, (halo_sems_0, halo_sems_1, halo_sems_2, halo_sems_3), where, counts)
     halo_s = Halo(so, sp, (slope_sems_0, slope_sems_1, slope_sems_2, slope_sems_3), where, counts)
@@ -220,10 +223,36 @@
     halo_x.fill_edges()
     halo_x.centre()
     halo_s.fill_edges()
+    g_ref[..., 0:channels] = g_raw[...]
+    g_ref[..., channels:] = jnp.zeros(g_ref.shape[:-1] + (spare,), jnp.bfloat16)
+    for raw, ready in ((inw_raw, inw_ref), (outw_raw, outw_ref)):
+        ready[0:channels, :] = raw[...]
+        ready[channels:, :] = jnp.zeros((spare, hidden), jnp.bfloat16)
+    taps_ref[...] = jnp.zeros_like(taps_ref)
+
+    def tap_rows(ij, _):
+        i, j = ij // K, ij % K
+        rows_k = kernel_ref[i, j].astype(jnp.float32)
+        for k in range(K):
+            taps_ref[j, k, i, :, 0:channels] = jnp.broadcast_to(
+                rows_k[k : k + 1, :], (SUB, channels)
+            )
+        return 0
+
+    lax.fori_loop(0, K * K, tap_rows, 0)
+    vec_ref[...] = jnp.zeros_like(vec_ref)
+    vec_ref[0:1, 0:channels] = bias_ref[...]
+    for half in range(2):
+        film = lax.dot_general(
+            report_ref[...], fw_ref[half * channels : (half + 1) * channels, :],
+            (((1,), (1,)), ((), ())), preferred_element_type=jnp.float32,
+        )
+        film = film + small_ref[half : half + 1, 0:channels]
+        vec_ref[half + 1 : half + 2, 0:channels] = film + (1.0 if half == 0 else 0.0)
     accw[...] = jnp.zeros_like(accw)
     accb[...] = jnp.zeros_like(accb)
     accf[...] = jnp.zeros_like(accf)
-    tail = row_of["end"] // SUB * SUB
+    tail = row_of["kernel"]
     part[tail:, :] = jnp.zeros((part.shape[0] - tail, LANES), jnp.float32)
     halo_x.relay()
     halo_x.finish()
@@ -240,6 +269,9 @@
     lax.fori_loop(0, crops, forward, 0)
 
     conv_bias, scale, shift = vec_ref[0:1, :], vec_ref[1:2, :], vec_ref[2:3, :]
+    in_bias = jnp.concatenate(
+        [small_ref[2 + b : 3 + b, :] for b in range(hidden // LANES)], axis=1
+    )
     real = lax.broadcasted_iota(jnp.int32, (1, LANES), 1) < channels
 
     def mlp(step, _):
@@ -253,16 +285,14 @@
         hidden_in = (normed * scale + shift).astype(jnp.bfloat16)
         grad = g_ref[crop, :, :, tile].astype(jnp.float32).reshape(voxels, LANES)
         grad = grad.astype(jnp.bfloat16)
-        pre = jnp.dot(hidden_in, inw_ref[...], preferred_element_type=jnp.float32) + inb_ref[...]
+        pre = jnp.dot(hidden_in, inw_ref[...], preferred_element_type=jnp.float32) + in_bias
         square = pre * pre
         th = jnp.tanh(GELU_C * (pre + 0.044715 * (square * pre)))
         act_low = (0.5 * pre * (1.0 + th)).astype(jnp.bfloat16)
         slope_act = 0.5 * (1.0 + th) + 0.5 * pre * (1.0 - th * th) * (
             GELU_C * (1.0 + (3.0 * 0.044715) * square)
         )
-        grad_act = lax.dot_general(
-            grad, outw_ref[...], (((1,), (1,)), ((), ())), preferred_element_type=jnp.float32
-        )
+        grad_act = jnp.dot(grad, outw_ref[...], preferred_element_type=jnp.float32)
         grad_pre = grad_act * slope_act
         grad_low = grad_pre.astype(jnp.bfloat16)
         grad_hidden = lax.dot_general(
@@ -311,7 +341,7 @@
             zero = jnp.zeros((SUB, LANES), jnp.float32)
             accs = lax.fori_loop(0, crops, gather, (zero,) * K)
             for i in range(K):
-                row = row_of["kernel"] + (i * K + j) * K + k
+                row = row_of["kernel"] + (i * K + j) * SUB + k
                 part[pl.ds(row, 1), :] = jnp.sum(accs[i], axis=0, keepdims=True)
         return 0
 
@@ -381,7 +411,8 @@
             for d in range(depth):
                 for h in range(rows):
                     grad = g_ref[crop, d, h, tile].astype(jnp.float32)
-                    gi_ref[crop, d, h, tile] = (grad + accs[d * rows + h]).astype(jnp.bfloat16)
+                    total_in = grad + accs[d * rows + h]
+                    gi_ref[crop, d, h, tile] = total_in[:, 0:channels].astype(jnp.bfloat16)
 
     def backward_loop(first, last):
         def step(crop, _):
@@ -408,7 +439,16 @@
         arrived(offset).wait_recv()
 
     each(settle)
-    red_ref[...] = full[...].astype(jnp.float32)
+    red_ref[...] = full[...].astype(jnp.float32) * factor
+    for name, out_ref in (("in", ginw_ref), ("out", goutw_ref)):
+        for block in range(hidden // LANES):
+            first = row_of[name] + block * channels
+            out_ref[:, block * LANES : (block + 1) * LANES] = red_ref[first : first + channels, :]
+    for ij in range(K * K):
+        first = row_of["kernel"] + ij * SUB
+        gk_ref[ij // K, ij % K] = red_ref[first : first + K, 0:channels]
+    gb_ref[...] = red_ref[row_of["small"] : row_of["small"] + 1, 0:channels]
+    gsmall_ref[...] = red_ref[row_of["small"] : row_of["small"] + SUB, :]
 
 
 def local(
@@ -421,25 +461,25 @@
     width = merged // channels
     tiles = width // SUB
     extra = LANES - channels
-    block = (crops, slices, lines, tiles, SUB, LANES)
+    block = (crops, slices, lines, tiles, SUB, channels)
+    wide_block = block[:-1] + (LANES,)
 
     def to_block(array):
-        array = array.reshape(crops, slices, lines, tiles, SUB, channels)
-        return jnp.pad(array, ((0, 0),) * 5 + ((0, extra),))
-
-    film = jnp.dot(report[None, :], film_weight, preferred_element_type=jnp.float32)[0] + film_bias
-    vecs = jnp.stack([conv_bias, 1.0 + film[:channels], film[channels:]])
-    vecs = jnp.pad(vecs, ((0, SUB - 3), (0, extra)))
-    taps = jnp.transpose(conv_kernel[:, 0].astype(jnp.float32), (2, 3, 1, 0))
-    taps = jnp.broadcast_to(
-        jnp.pad(taps, ((0, 0),) * 3 + ((0, extra),))[:, :, :, None, :], (K, K, K, SUB, LANES)
+        return array.reshape(block)
+
+    smalls = jnp.concatenate(
+        [
+            jnp.pad(film_bias.reshape(2, channels), ((0, 0), (0, extra))),
+            in_bias.reshape(hidden // LANES, LANES),
+        ]
     )
+    raw_kernel = jnp.transpose(conv_kernel[:, 0], (1, 2, 3, 0))
     total = counts[0] * counts[1] * counts[2]
     blocks = hidden // LANES
     row_of = {"in": 0, "out": blocks * channels, "kernel": 2 * blocks * channels}
-    row_of["small"] = row_of["kernel"] + TAPS
+    row_of["small"] = row_of["kernel"] + K * K * SUB
     row_of["in_bias"] = row_of["small"] + 3
-    row_of["end"] = row_of["in_bias"] + blocks
+    row_of["end"] = row_of["in_bias"] + -(-(blocks + 3) // SUB) * SUB
     unit = 16 * total
     all_rows = -(-row_of["end"] // unit) * unit
     chunk = all_rows // total
@@ -447,21 +487,33 @@
     bf, f32 = jnp.bfloat16, jnp.float32
     dma = pltpu.SemaphoreType.DMA
     halo_sems = [dma((len(DIRS),))] * 2 + [dma((2, len(DIRS) + 1))] * 2
-    grad_input, red = pl.pallas_call(
-        functools.partial(kernel, counts, channels, row_of),
+    factor = 1.0 / math.sqrt(crops * slices * lines * width * total)
+    grad_input, grad_kernel, grad_bias, smalls_out, grad_in_w, grad_out_w = pl.pallas_call(
+        functools.partial(kernel, counts, channels, row_of, factor),
         out_shape=(
             jax.ShapeDtypeStruct(block, bf),
-            jax.ShapeDtypeStruct((all_rows, LANES), f32),
+            jax.ShapeDtypeStruct((K, K, K, channels), f32),
+            jax.ShapeDtypeStruct((1, channels), f32),
+            jax.ShapeDtypeStruct((SUB, LANES), f32),
+            jax.ShapeDtypeStruct((channels, hidden), f32),
+            jax.ShapeDtypeStruct((channels, hidden), f32),
         ),
-        in_specs=[pl.BlockSpec(memory_space=pltpu.VMEM)] * 7,
-        out_specs=(pl.BlockSpec(memory_space=pltpu.VMEM),) * 2,
+        in_specs=[pl.BlockSpec(memory_space=pltpu.VMEM)] * 9,
+        out_specs=(pl.BlockSpec(memory_space=pltpu.VMEM),) * 6,
         scratch_shapes=[
+            pltpu.VMEM(wide_block, bf),
+            pltpu.VMEM(wide_block, bf),
+            pltpu.VMEM((K, K, K, SUB, LANES), f32),
+            pltpu.VMEM((LANES, hidden), bf),
+            pltpu.VMEM((LANES, hidden), bf),
+            pltpu.VMEM((all_rows, LANES), f32),
             pltpu.VMEM(padded, bf),
             pltpu.VMEM(padded, bf),
-            pltpu.VMEM(block, bf),
+            pltpu.VMEM(wide_block, bf),
             pltpu.VMEM(padded[:3] + (padded[3] * SUB, LANES), f32),
             pltpu.VMEM((crops * tiles, slices, lines, SUB, LANES), f32),
             pltpu.VMEM((crops * tiles, slices, lines, SUB, LANES), f32),
+            pltpu.VMEM((SUB, LANES), f32),
             pltpu.VMEM((2, LANES, hidden), f32),
             pltpu.VMEM((SUB, hidden), f32),
             pltpu.VMEM((SUB, LANES), f32),
@@ -481,28 +533,21 @@
     )(
         to_block(volume),
         to_block(grad_out),
-        taps,
-        vecs,
-        jnp.pad(in_weight, ((0, extra), (0, 0))),
-        in_bias[None, :],
-        jnp.pad(out_weight, ((0, 0), (0, extra))),
+        raw_kernel,
+        conv_bias[None, :],
+        report[None, :],
+        film_weight.T,
+        smalls,
+        in_weight,
+        out_weight.T,
     )
-    grad_input = grad_input[..., :channels].reshape(volume.shape)
-    factor = 1.0 / math.sqrt(crops * slices * lines * width * total)
-    red = red * factor
-
-    def matrix(name):
-        rows = red[row_of[name] : row_of[name] + blocks * channels, :]
-        return rows.reshape(blocks, channels, LANES)
-
-    grad_in_w = jnp.transpose(matrix("in"), (1, 0, 2)).reshape(channels, hidden)
-    grad_out_w = jnp.transpose(matrix("out")[:, :, :], (0, 2, 1)).reshape(hidden, channels)
-    grad_kernel = red[row_of["kernel"] : row_of["kernel"] + TAPS, :channels].T
-    grad_kernel = grad_kernel.reshape(channels, 1, K, K, K)
-    small = red[row_of["small"] : row_of["small"] + 3, :channels]
-    grad_film = jnp.concatenate([small[1], small[2]])
-    grad_in_b = red[row_of["in_bias"] : row_of["in_bias"] + blocks, :].reshape(hidden)
-    return grad_input, grad_kernel, small[0], grad_film, grad_in_w, grad_in_b, grad_out_w
+    grad_input = grad_input.reshape(volume.shape)
+    grad_kernel = jnp.transpose(grad_kernel, (3, 0, 1, 2))[:, None]
+    grad_film = smalls_out[1:3, :channels].reshape(2 * channels)
+    grad_in_b = smalls_out[3 : 3 + blocks].reshape(hidden)
+    return (
+        grad_input, grad_kernel, grad_bias[0], grad_film, grad_in_w, grad_in_b, grad_out_w.T
+    )
 
 
 def solution(mesh):

time: 81.6 us -> 74.4 us (0.912)
  other arithmetic: 4.72 us -> 0.6 us
  local copies, waits for them, and re-layouts: 13.3 us -> 10.4 us
    pad x5 -> x0, local copies, waits for them, and re-layouts: 3.77 us -> none  [the longest x1 1.53 us: local(): jnp.pad(in_weight, ((0, extra), (0, 0)))]
    unnamed x8 -> x22, local copies, waits for them, and re-layouts: 1.7 us -> 3.76 us
    broadcast_in_dim x2 -> x1, local copies, waits for them, and re-layouts: 2.52 us -> 0.58 us  [local(): report[None, :]]
    reshape x8 -> x6, local copies, waits for them, and re-layouts: 4.73 us -> 6.08 us  [the longest x2 2.83 us: to_block(): return array.reshape(block)]
    another operation x2 -> x0, other arithmetic: 1.33 us -> none  [local(): vecs = jnp.stack([conv_bias, 1.0 + film[:channels], film[channels:]])]
    mul x1 -> x0, other arithmetic: 1.08 us -> none  [local(): red = red * factor]
    pad x1 -> x0, other arithmetic: 0.92 us -> none  [local(): jnp.pad(taps, ((0, 0),) * 3 + ((0, extra),))[:, :, :, None, :]]
where the time goes in v2:
time: 74.4 us; the launch traced here: 74.1 us
  Pallas kernels  62.4 us (84%)
  local copies, waits for them, and re-layouts  10.4 us (14%)
    pallas_call x1, Pallas kernels, local(): pl.pallas_call(functools.partial(kernel, counts, channels, row_of, factor...  62.4 us
    unnamed x22, local copies, waits for them, and re-layouts  3.76 us
    reshape x2, local copies, waits for them, and re-layouts, to_block(): return array.reshape(block)  2.83 us
    reshape x1, local copies, waits for them, and re-layouts, local(): grad_input = grad_input.reshape(volume.shape)  1.94 us

profile of v2, /device:TPU:1, one launch (start us, length us, event | category | flops | bytes accessed | tf_op | source)
XLA Modules:
  0.0 74.1 jit_solution(11438414204358472148)
XLA Ops:
  0.6 0.0 copy-start.7
  0.6 0.0 copy-start.5
  0.7 0.7 copy-done.7
  1.3 0.1 reshape.37
  1.4 0.0 copy-done.5
  1.4 0.0 copy-start.6
  1.4 0.6 select_maximum_fusion.small_ref
  2.0 0.1 copy-done.6
  2.1 0.6 broadcast_in_dim.10.report_ref
  2.7 0.0 copy-start.1
  2.7 1.9 %reshape.35.x_raw = bf16[2,4,8,2,8,96]{5,4,3,2,1,0:T(8,128)(2,1)} reshape(bf16[2,4,8,1536]{3,2,1,0:T(8,128)(2,1)} %param.10) | data formatting | bytes 393216 | tf_op jit(solution)/shard_map/reshape | solution.py:468
  4.6 0.0 copy-done.1
  4.6 0.9 %reshape.36.g_raw = bf16[2,4,8,2,8,96]{5,4,3,2,1,0:T(8,128)(2,1)} reshape(bf16[2,4,8,1536]{3,2,1,0:T(8,128)(2,1)S(1)} %copy-done.1) | data formatting | bytes 393216 | tf_op jit(solution)/shard_map/reshape | solution.py:468
  5.5 62.4 %block.1 = (bf16[2,4,8,2,8,96]{5,4,3,2,1,0:T(8,128)(2,1)}, f32[7,7,7,96]{3,2,1,0:T(8,128)}, f32[1,96]{1,0:T(1,128)}, f32[8,128]{1,0:T(8,128)}, f32[96,384]{1,0:T(8,128)}, /*index=5*/f32[96,384]{1,0:T(8,128)}) custom-call(bf16[2,4,8,2,8,96]{5,4,3,2,1,0:T(8,128)(2,1)} %reshape.35.x_raw, bf16[2,4,8,2,8,96]{5,4,3,2,1,0:T(8,128)(2,1)} %reshape.36.g_raw, ...), custom_call_target="tpu_custom_call" | custom-call | tf_op jit(solution)/shard_map/block/pallas_call | solution.py:491
  68.0 0.0 copy-start
  68.0 1.9 %reshape.39 = bf16[2,4,8,1536]{3,2,1,0:T(8,128)(2,1)} reshape(bf16[2,4,8,2,8,96]{5,4,3,2,1,0:T(8,128)(2,1)} %get-tuple-element.13) | data formatting | bytes 393216 | tf_op jit(solution)/shard_map/reshape | solution.py:544
  69.9 0.0 copy-done
  69.9 0.0 copy-start.4
  69.9 0.0 copy-start.3
  69.9 0.9 %copy.17 = f32[96,1,7,7,7]{0,1,4,3,2:T(1,128)} copy(f32[96,1,7,7,7]{0,4,3,2,1:T(8,128)S(1)} %bitcast.21) | data formatting | bytes 263424
  70.8 0.0 copy-done.4
  70.8 0.6 slice_bitcast_fusion
  71.3 0.0 copy-start.8
  71.4 0.6 reshape.40
  72.0 0.0 copy-done.8
  72.0 0.5 copy.21
  72.5 0.0 copy-done.3
  72.5 0.0 copy-start.2
  72.5 0.7 copy.22
  73.2 0.3 copy-done.2
  73.5 0.7 copy.23
  (1 shorter events, 0.0 us)
Async XLA Ops:
  0.6 0.7 copy-start.7
  0.6 0.8 %copy-start.5 = (f32[384]{0:T(512)S(1)}, f32[384]{0:T(512)}, u32[]{:S(2)}) copy-start(f32[384]{0:T(512)} %param.18) | copy-start | bytes 4612
  1.4 0.7 copy-start.6
  2.7 1.9 %copy-start.1 = (bf16[2,4,8,1536]{3,2,1,0:T(8,128)(2,1)S(1)}, bf16[2,4,8,1536]{3,2,1,0:T(8,128)(2,1)}, u32[]{:S(2)}) copy-start(bf16[2,4,8,1536]{3,2,1,0:T(8,128)(2,1)} %param.11) | copy-start | bytes 589828
  68.0 2.0 %copy-start = (f32[7,7,7,96]{3,2,1,0:T(8,128)S(1)}, f32[7,7,7,96]{3,2,1,0:T(8,128)}, u32[]{:S(2)}) copy-start(f32[7,7,7,96]{3,2,1,0:T(8,128)} %get-tuple-element.14) | copy-start | bytes 395140
  69.9 0.9 %copy-start.4 = (f32[8,128]{1,0:T(8,128)S(1)}, f32[8,128]{1,0:T(8,128)}, u32[]{:S(2)}) copy-start(f32[8,128]{1,0:T(8,128)} %get-tuple-element.16) | copy-start | bytes 12292
  69.9 2.6 %copy-start.3 = (f32[96,384]{1,0:T(8,128)S(1)}, f32[96,384]{1,0:T(8,128)}, u32[]{:S(2)}) copy-start(f32[96,384]{1,0:T(8,128)} %get-tuple-element.37) | copy-start | bytes 442372
  71.3 0.6 copy-start.8
  72.5 1.0 %copy-start.2 = (f32[96,384]{1,0:T(8,128)S(1)}, f32[96,384]{1,0:T(8,128)}, u32[]{:S(2)}) copy-start(f32[96,384]{1,0:T(8,128)} %get-tuple-element.18) | copy-start | bytes 442372
